TPU v7x, 32 devices: a whole 2x2x4 slice. The times are simulated.
32 devices in a mesh: fsdp: 8 (over z, x), tensor: 4 (over y, core).
Axes of the slice: x: 2, y: 2, z: 4, core: 2. Of those that a mesh axis runs over, the one named last changes fastest.
Arguments:
- hidden_in: bfloat16 [4096, 2048], P(('fsdp', 'tensor')), may hold values from -6 to 6
- ln_gain: float32 [2048], replicated, may hold values from 0.5 to 1.5
- ln_bias: float32 [2048], replicated, may hold values from -1.75 to 1.75
- w_qkv: bfloat16 [2048, 3, 2048], P('fsdp', None, 'tensor'), may hold values from -0.125 to 0.125
- b_qkv: float32 [3, 2048], P(None, 'tensor'), may hold values from -1.75 to 1.75
- w_dense: bfloat16 [2048, 2048], P('tensor', 'fsdp'), may hold values from -0.5 to 0.5
- b_dense: float32 [2048], replicated, may hold values from -1.75 to 1.75
- w_fc1: bfloat16 [2048, 8192], P('fsdp', 'tensor'), may hold values from -0.125 to 0.125
- b_fc1: float32 [8192], P('tensor'), may hold values from -1.75 to 1.75
- w_fc2: bfloat16 [8192, 2048], P('tensor', 'fsdp'), may hold values from -0.0625 to 0.0625
- b_fc2: float32 [2048], replicated, may hold values from -1.75 to 1.75
- segment_ids: int32 [8, 512], P('fsdp'), may hold values from 0 to 7, never falling along the last dimension, each value on 1 to 256 neighbouring positions
- out_grad: bfloat16 [4096, 2048], P(('fsdp', 'tensor')), may hold values from -6 to 6
Outputs:
- hidden_out: bfloat16 [4096, 2048], P(('fsdp', 'tensor'))
- input_grad: float32 [4096, 2048], P(('fsdp', 'tensor'))
- ln_gain_grad: float32 [2048], replicated
- ln_bias_grad: float32 [2048], replicated
- w_qkv_grad: float32 [2048, 3, 2048], P('fsdp', None, 'tensor')
- b_qkv_grad: float32 [3, 2048], P(None, 'tensor')
- w_dense_grad: float32 [2048, 2048], P('tensor', 'fsdp')
- b_dense_grad: float32 [2048], replicated
- w_fc1_grad: float32 [2048, 8192], P('fsdp', 'tensor')
- b_fc1_grad: float32 [8192], P('tensor')
- w_fc2_grad: float32 [8192, 2048], P('tensor', 'fsdp')
- b_fc2_grad: float32 [2048], replicated
Inputs may be any that keep to these rules, and one draw needn't show every extreme that they name: `segment_ids`: in each sequence the document numbers never fall; each document has 1 to 256 tokens and one has exactly 256.
All inputs are finite; a program needn't handle non-finite values.
Results may differ from a plain program's by a relative error of at most 0.0093.
Values may be sent and summed in bfloat16 or wider, within the bound.
No kernel may reach another device: no remote copies, remote signals or barrier semaphores. Data moves between devices by JAX's collectives and lax.ppermute only.
A program may use at most 192 MiB of HBM per device.

v0:
```python
import math
import jax
import jax.numpy as jnp
from jax import lax
from jax.sharding import PartitionSpec as P

HEAD_DIM = 64
ROT = 32
EPS = 1e-05


def layer_norm(values, norm_gain, norm_shift):
    centred = values - jnp.mean(values, axis=-1, keepdims=True)
    variance = jnp.mean(centred * centred, axis=-1, keepdims=True)
    return centred * lax.rsqrt(variance + EPS) * norm_gain + norm_shift


def gelu_tanh(values):
    return jax.nn.gelu(values, approximate=True)


def rotary_tables(length):
    positions = jnp.arange(length).astype(jnp.float32)
    inverse = 10000.0 ** (-jnp.arange(0, ROT, 2).astype(jnp.float32) / ROT)
    angles = positions[:, None] * inverse[None, :]
    return (jnp.cos(angles), jnp.sin(angles))


def rotate(values, cosine_rows, sine_rows):
    half_rot = ROT // 2
    first_half = values[..., :half_rot]
    second = values[..., half_rot:ROT]
    others = values[..., ROT:]
    cos_rows = cosine_rows[:, None, :]
    sin_rows = sine_rows[:, None, :]
    return jnp.concatenate(
        [
            first_half * cos_rows - second * sin_rows,
            second * cos_rows + first_half * sin_rows,
            others,
        ],
        axis=-1,
    )


def unrotate(values, cosine_rows, sine_rows):
    half_rot = ROT // 2
    first_half = values[..., :half_rot]
    second = values[..., half_rot:ROT]
    others = values[..., ROT:]
    cos_rows = cosine_rows[:, None, :]
    sin_rows = sine_rows[:, None, :]
    return jnp.concatenate(
        [
            first_half * cos_rows + second * sin_rows,
            second * cos_rows - first_half * sin_rows,
            others,
        ],
        axis=-1,
    )


def contract_rows(left, right):
    return lax.dot_general(
        left, right, (((0,), (0,)), ((), ())), preferred_element_type=jnp.float32
    )


def contract_cols(left, right):
    return lax.dot_general(
        left, right, (((1,), (1,)), ((), ())), preferred_element_type=jnp.float32
    )


def body(
    hidden_in,
    ln_gain,
    ln_bias,
    w_qkv,
    b_qkv,
    w_dense,
    b_dense,
    w_fc1,
    b_fc1,
    w_fc2,
    b_fc2,
    segment_ids,
    out_grad,
):
    hidden = hidden_in.astype(jnp.float32)
    normed = layer_norm(hidden, ln_gain, ln_bias)
    normed_all = lax.all_gather(normed.astype(jnp.bfloat16), "tensor", axis=0, tiled=True)
    seq_len = normed_all.shape[0]
    qkv_weights, up_weights = (
        lax.all_gather(w_qkv, "fsdp", axis=0, tiled=True),
        lax.all_gather(w_fc1, "fsdp", axis=0, tiled=True),
    )
    local_width = b_qkv.shape[1]
    head_count = local_width // HEAD_DIM
    mixed_proj = (
        jnp.einsum("sd,djc->sjc", normed_all, qkv_weights, preferred_element_type=jnp.float32)
        + b_qkv
    )
    before = jnp.dot(normed_all, up_weights, preferred_element_type=jnp.float32) + b_fc1
    cosine_rows, sine_rows = rotary_tables(seq_len)
    split_heads = mixed_proj.reshape(seq_len, 3, head_count, HEAD_DIM)
    queries = rotate(split_heads[:, 0], cosine_rows, sine_rows).astype(jnp.bfloat16)
    key_rows = rotate(split_heads[:, 1], cosine_rows, sine_rows).astype(jnp.bfloat16)
    value_rows = split_heads[:, 2].astype(jnp.bfloat16)
    segments = segment_ids[0]
    block_rows = min(512, seq_len)
    block_count = seq_len // block_rows
    score_scale = 1.0 / math.sqrt(HEAD_DIM)
    col_pos = jnp.arange(seq_len, dtype=jnp.int32)

    def block_scores(offset):
        row_pos = offset + jnp.arange(block_rows, dtype=jnp.int32)
        allowed = (col_pos[None, :] <= row_pos[:, None]) & (segments[:, None] == segments[None, :])
        scores = (
            jnp.einsum("qhd,khd->hqk", queries, key_rows, preferred_element_type=jnp.float32)
            * score_scale
        )
        return (queries, jnp.where(allowed[None], scores, -1e30))

    def forward_block(block_index):
        offset = block_index * block_rows
        query_rows, scores = block_scores(offset)
        highest = jnp.max(scores, axis=-1, keepdims=True)
        shifted = jnp.exp(scores - highest)
        totals = jnp.sum(shifted, axis=-1, keepdims=True)
        attend = (shifted / totals).astype(jnp.bfloat16)
        context = jnp.einsum("hqk,khd->qhd", attend, value_rows, preferred_element_type=jnp.float32)
        return (context, (highest + jnp.log(totals))[..., 0])

    contexts, log_sums = lax.map(forward_block, jnp.arange(block_count, dtype=jnp.int32))
    context_b = contexts.reshape(seq_len, local_width).astype(jnp.bfloat16)
    activated_b = gelu_tanh(before).astype(jnp.bfloat16)
    out_weights, down_weights = (
        lax.all_gather(w_dense, "fsdp", axis=1, tiled=True),
        lax.all_gather(w_fc2, "fsdp", axis=1, tiled=True),
    )
    attn_part = jnp.dot(context_b, out_weights, preferred_element_type=jnp.float32)
    mlp_part = jnp.dot(activated_b, down_weights, preferred_element_type=jnp.float32)
    branch_total = lax.psum_scatter(
        attn_part, "tensor", scatter_dimension=0, tiled=True
    ) + lax.psum_scatter(
        mlp_part.astype(jnp.bfloat16), "tensor", scatter_dimension=0, tiled=True
    ).astype(
        jnp.float32
    )
    hidden_out = (hidden + branch_total + b_dense + b_fc2).astype(jnp.bfloat16)
    grad_all = lax.all_gather(out_grad, "tensor", axis=0, tiled=True)
    dense_grad_local = contract_rows(context_b, grad_all)
    down_grad_local = contract_rows(activated_b, grad_all)
    dense_weight_grad, down_weight_grad = (
        lax.psum_scatter(dense_grad_local, "fsdp", scatter_dimension=1, tiled=True),
        lax.psum_scatter(down_grad_local, "fsdp", scatter_dimension=1, tiled=True),
    )
    context_grad = contract_cols(grad_all, out_weights).astype(jnp.bfloat16)
    activated_grad = contract_cols(grad_all, down_weights)
    gelu_value, gelu_pull = jax.vjp(gelu_tanh, before)
    before_grad = gelu_pull(activated_grad)[0].astype(jnp.bfloat16)
    up_grad_local = contract_rows(normed_all, before_grad)
    context_heads = context_grad.reshape(seq_len, head_count, HEAD_DIM)

    def backward_block(accumulate, block_index):
        key_acc, value_acc = accumulate
        offset = block_index * block_rows
        query_rows, scores = block_scores(offset)
        log_sum = lax.dynamic_index_in_dim(log_sums, block_index, 0, keepdims=False)
        attend = jnp.exp(scores - log_sum[..., None])
        attend_grad = jnp.einsum(
            "qhd,khd->hqk", context_heads, value_rows, preferred_element_type=jnp.float32
        )
        row_inner = jnp.sum(attend * attend_grad, axis=-1, keepdims=True)
        score_grad = (attend * (attend_grad - row_inner)).astype(jnp.bfloat16)
        query_grad = (
            jnp.einsum("hqk,khd->qhd", score_grad, key_rows, preferred_element_type=jnp.float32)
            * score_scale
        )
        key_acc = (
            key_acc
            + jnp.einsum("hqk,qhd->khd", score_grad, query_rows, preferred_element_type=jnp.float32)
            * score_scale
        )
        value_acc = value_acc + jnp.einsum(
            "hqk,qhd->khd",
            attend.astype(jnp.bfloat16),
            context_heads,
            preferred_element_type=jnp.float32,
        )
        return ((key_acc, value_acc), query_grad)

    zero_heads = jnp.zeros((seq_len, head_count, HEAD_DIM), jnp.float32)
    (key_grad, value_grad), query_grads = lax.scan(
        backward_block, (zero_heads, zero_heads), jnp.arange(block_count, dtype=jnp.int32)
    )
    query_grad = query_grads.reshape(seq_len, head_count, HEAD_DIM)
    mixed_grad = jnp.stack(
        [
            unrotate(query_grad, cosine_rows, sine_rows),
            unrotate(key_grad, cosine_rows, sine_rows),
            value_grad,
        ],
        axis=1,
    )
    mixed_grad = mixed_grad.reshape(seq_len, 3, local_width).astype(jnp.bfloat16)
    qkv_grad_local = jnp.einsum(
        "sd,sjc->djc", normed_all, mixed_grad, preferred_element_type=jnp.float32
    )
    attn_back = jnp.einsum(
        "sjc,djc->sd", mixed_grad, qkv_weights, preferred_element_type=jnp.float32
    )
    mlp_back = contract_cols(before_grad, up_weights)
    normed_grad = lax.psum_scatter(
        attn_back, "tensor", scatter_dimension=0, tiled=True
    ) + lax.psum_scatter(
        mlp_back.astype(jnp.bfloat16), "tensor", scatter_dimension=0, tiled=True
    ).astype(
        jnp.float32
    )
    norm_value, norm_pull = jax.vjp(layer_norm, hidden, ln_gain, ln_bias)
    hidden_grad, gain_local, shift_local = norm_pull(normed_grad)
    cotangent = out_grad.astype(jnp.float32)
    input_grad = cotangent + hidden_grad
    gain_grad, shift_grad, out_bias_grad = lax.psum(
        (gain_local, shift_local, jnp.sum(cotangent, axis=0)), ("fsdp", "tensor")
    )
    qkv_bias_grad, up_bias_grad = lax.psum(
        (
            jnp.sum(mixed_grad, axis=0, dtype=jnp.float32),
            jnp.sum(before_grad, axis=0, dtype=jnp.float32),
        ),
        "fsdp",
    )
    qkv_weight_grad, up_weight_grad = (
        lax.psum_scatter(qkv_grad_local, "fsdp", scatter_dimension=0, tiled=True),
        lax.psum_scatter(up_grad_local, "fsdp", scatter_dimension=0, tiled=True),
    )
    return (
        hidden_out,
        input_grad,
        gain_grad,
        shift_grad,
        qkv_weight_grad,
        qkv_bias_grad,
        dense_weight_grad,
        out_bias_grad,
        up_weight_grad,
        up_bias_grad,
        down_weight_grad,
        out_bias_grad,
    )


def solution(mesh):
    in_specs = (
        P(("fsdp", "tensor"), None),
        P(),
        P(),
        P("fsdp", None, "tensor"),
        P(None, "tensor"),
        P("tensor", "fsdp"),
        P(),
        P("fsdp", "tensor"),
        P("tensor"),
        P("tensor", "fsdp"),
        P(),
        P("fsdp", None),
        P(("fsdp", "tensor"), None),
    )
    out_specs = (
        P(("fsdp", "tensor"), None),
        P(("fsdp", "tensor"), None),
        P(),
        P(),
        P("fsdp", None, "tensor"),
        P(None, "tensor"),
        P("tensor", "fsdp"),
        P(),
        P("fsdp", "tensor"),
        P("tensor"),
        P("tensor", "fsdp"),
        P(),
    )
    return jax.shard_map(body, mesh=mesh, in_specs=in_specs, out_specs=out_specs, check_vma=False)
```

profile of v0, /device:TPU:0, one launch (start us, length us, event | category | flops | bytes accessed | tf_op | source)
XLA Modules:
  0.0 1531.4 jit_solution(14621272679159537273)
XLA Ops:
  7.2 0.7 all-gather.17.cloned.1.call-update
  8.0 0.7 all-gather.11.cloned.1.call-update
  8.7 1.2 convert_reduce_fusion.2
  9.9 1.3 fusion.35
  11.3 0.5 copy-done.36
  11.8 0.5 copy-done.34
  12.3 2.3 fusion.33
  14.6 2.3 copy.25
  17.0 0.5 all-gather.13.cloned.1.call-update
  17.6 0.5 all-gather.15.cloned.1.call-update
  18.2 0.8 multiply_cosine_fusion
  19.0 0.9 fusion.40
  19.9 15.0 all-gather.17.cloned.1.call-done
  34.9 53.2 %all-gather.11.cloned.1.call-done = bf16[512,2048]{1,0:T(8,128)(2,1)} async-done(((bf16[512,256]{1,0:T(8,128)(2,1)}), bf16[512,2048]{1,0:T(8,128)(2,1)}) %all-gather.11.cloned.1.call-update) | async-done | bytes 2097168 | tf_op jit(solution)/shard_map/all_gather | solution.py:139
  88.1 4.3 convolution_convert_fusion.2
  92.4 18.7 %all-gather.7.cloned.1.call-done = bf16[512,2048]{1,0:T(8,128)(2,1)} async-done(((bf16[128,2048]{1,0:T(8,128)(2,1)}), bf16[512,2048]{1,0:T(8,128)(2,1)}) %all-gather.7.cloned.1.call-update) | async-done | bytes 2097168 | tf_op jit(solution)/shard_map/all_gather | solution.py:92
  111.1 102.4 %all-gather.9.cloned.1.call-done = bf16[2048,3,512]{0,2,1:T(8,128)(2,1)} async-done(((bf16[256,3,512]{0,2,1:T(8,128)(2,1)}), bf16[2048,3,512]{0,2,1:T(8,128)(2,1)}) %all-gather.9.cloned.1.call-update) | async-done | bytes 6291472 | tf_op jit(solution)/shard_map/all_gather | solution.py:95
  213.5 6.7 fusion.17
  220.5 0.4 copy-done.17
  221.2 0.6 copy-done.11
  221.9 4.7 fusion.53
  226.6 111.9 %all-gather.13.cloned.1.call-done = bf16[2048,2048]{1,0:T(8,128)(2,1)} async-done(((bf16[256,2048]{1,0:T(8,128)(2,1)}), bf16[2048,2048]{1,0:T(8,128)(2,1)}) %all-gather.13.cloned.1.call-update) | async-done | bytes 8388624 | tf_op jit(solution)/shard_map/all_gather | solution.py:96
  338.5 10.5 fusion.55
  349.0 115.0 %all-gather.15.cloned.1.call-done = bf16[2048,2048]{1,0:T(8,128)(2,1)} async-done(((bf16[2048,256]{1,0:T(8,128)(2,1)}), bf16[2048,2048]{1,0:T(8,128)(2,1)}) %all-gather.15.cloned.1.call-update) | async-done | bytes 8388624 | tf_op jit(solution)/shard_map/all_gather | solution.py:140
  464.0 12.8 convert_reduce_fusion
  476.9 1.3 copy-done.41
  478.2 5.9 convolution_convert_fusion
  484.2 4.7 fusion
  489.0 1.4 log_add_fusion
  490.3 0.2 copy-done
  490.6 3.3 fusion.27
  493.9 2.0 copy.32
  496.0 4.6 multiply_reduce_fusion
  500.6 4.5 multiply_convert_fusion
  505.2 0.8 fusion.25
  506.1 1.4 fusion.24
  507.7 1.0 pad_maximum_fusion.3
  508.7 2.0 copy.30
  510.8 2.1 copy.31
  512.8 8.8 convolution_bitcast_fusion
  521.7 0.3 reduce-scatter.11.cloned.1.call-start
  521.9 0.4 copy-done.40
  522.3 11.8 convolution_convert_fusion.1
  534.2 5.0 fusion.26
  539.2 0.8 copy-done.7
  540.0 3.2 fusion.54
  543.3 0.9 copy-done.8
  544.3 4.8 fusion.56
  549.2 8.1 fusion.13
  557.4 0.3 reduce-scatter.23.cloned.1.call-start
  557.7 14.1 fusion.50
  571.9 12.8 fusion.57
  585.0 0.4 copy-done.32
  585.3 35.0 %all-reduce.1 = (f32[3,512]{1,0:T(4,128)}, f32[2048]{0:T(1024)}) all-reduce(f32[3,512]{1,0:T(4,128)S(1)} %convert_reduce_fusion.1, f32[2048]{0:T(1024)S(1)} %copy-done.32), channel_id=1, replica_groups=mesh['fsdp'=8,'tensor'=4] {'fsdp'}, use_global_device_ids=true, to_apply=%region_17.18 | all-reduce | flops 3584 | bytes 28672 | tf_op jit(solution)/shard_map/psum | solution.py:229
  620.4 1.8 fusion.34
  622.3 23.2 %reduce-scatter.9.cloned.1.call-done = f32[128,2048]{1,0:T(8,128)} async-done(((f32[512,2048]{1,0:T(8,128)}), f32[128,2048]{1,0:T(8,128)}) %reduce-scatter.9.cloned.1.call-update) | async-done | bytes 1048592 | tf_op jit(solution)/shard_map/reduce_scatter | solution.py:144
  645.4 3.2 fusion.52
  648.7 1.2 convert_reduce_fusion.3
  649.9 41.7 %all-reduce = (f32[2048]{0:T(1024)}, f32[2048]{0:T(1024)}, f32[2048]{0:T(1024)S(1)}) all-reduce(f32[2048]{0:T(1024)S(1)} %get-tuple-element.58, f32[2048]{0:T(1024)S(1)} %get-tuple-element.60, f32[2048]{0:T(1024)S(1)} %get-tuple-element.91), channel_id=1, replica_groups=mesh['fsdp'=8,'tensor'=4] {'fsdp','tensor'}, use_global_device_ids=true, to_apply=%region_12.13 | all-reduce | flops 6144 | bytes 49152 | tf_op jit(solution)/shard_map/psum | solution.py:226
  691.6 47.6 %reduce-scatter.19.cloned.1.call-done = f32[512,256]{1,0:T(8,128)} async-done(((f32[512,2048]{1,0:T(8,128)}), f32[512,256]{1,0:T(8,128)}) %reduce-scatter.19.cloned.1.call-update) | async-done | bytes 524304 | tf_op jit(solution)/shard_map/reduce_scatter | solution.py:156
  739.2 212.0 %reduce-scatter.17.cloned.1.call-done = f32[256,3,512]{2,0,1:T(8,128)} async-done(((f32[2048,3,512]{2,0,1:T(8,128)}), f32[256,3,512]{2,0,1:T(8,128)}) %reduce-scatter.17.cloned.1.call-update) | async-done | bytes 1572880 | tf_op jit(solution)/shard_map/reduce_scatter | solution.py:237
  951.2 286.7 %reduce-scatter.23.cloned.1.call-done = f32[2048,256]{1,0:T(8,128)} async-done(((f32[2048,2048]{1,0:T(8,128)}), f32[2048,256]{1,0:T(8,128)}) %reduce-scatter.23.cloned.1.call-update) | async-done | bytes 2097168 | tf_op jit(solution)/shard_map/reduce_scatter | solution.py:157
  1237.9 286.0 %reduce-scatter.21.cloned.1.call-done = f32[256,2048]{1,0:T(8,128)} async-done(((f32[2048,2048]{1,0:T(8,128)}), f32[256,2048]{1,0:T(8,128)}) %reduce-scatter.21.cloned.1.call-update) | async-done | bytes 2097168 | tf_op jit(solution)/shard_map/reduce_scatter | solution.py:238
  1523.9 0.6 copy.43
  (113 shorter events, 2.0 us)
Async XLA Ops:
  7.2 11.8 copy-start.31
  7.2 27.7 %all-gather.17.cloned.1.call-start = ((), (), s32[]{:S(2)}) async-start(), calls=%async_computation.15 | async-start | bytes 2621440 | tf_op jit(solution)/shard_map/all_gather | solution.py:152
  7.9 80.2 %all-gather.11.cloned.1.call-start = ((), (), s32[]{:S(2)}) async-start(), calls=%async_computation.10 | async-start | bytes 2359296 | tf_op jit(solution)/shard_map/all_gather | solution.py:139
  8.7 102.4 %all-gather.7.cloned.1.call-start = ((), (), s32[]{:S(2)}) async-start(), calls=%async_computation.8 | async-start | bytes 2621440 | tf_op jit(solution)/shard_map/all_gather | solution.py:92
  9.9 1.9 copy-start.27
  11.3 0.5 copy-start.36
  11.8 0.5 copy-start.34
  14.6 198.9 %all-gather.9.cloned.1.call-start = ((), (), s32[]{:S(2)}) async-start(), calls=%async_computation.9 | async-start | bytes 7077888 | tf_op jit(solution)/shard_map/all_gather | solution.py:95
  16.9 321.6 %all-gather.13.cloned.1.call-start = ((), (), s32[]{:S(2)}) async-start(), calls=%async_computation.12 | async-start | bytes 9437184 | tf_op jit(solution)/shard_map/all_gather | solution.py:96
  17.5 196.0 %copy-start.39 = (f32[3,512]{1,0:T(4,128)S(1)}, f32[3,512]{1,0:T(4,128)}, u32[]{:S(2)}) copy-start(f32[3,512]{1,0:T(4,128)} %param.17) | copy-start | bytes 18436
  17.5 446.5 %all-gather.15.cloned.1.call-start = ((), (), s32[]{:S(2)}) async-start(), calls=%async_computation.13 | async-start | bytes 9437184 | tf_op jit(solution)/shard_map/all_gather | solution.py:140
  18.1 602.2 %reduce-scatter.15.cloned.1.call-start = ((), (), s32[]{:S(2)}) async-start(), calls=%async_computation.17 | async-start | bytes 2621440 | tf_op jit(solution)/shard_map/reduce_scatter | solution.py:217
  220.2 0.8 copy-start.17
  220.2 0.8 copy-start.19
  220.2 1.7 copy-start.21
  220.5 0.7 copy-start.9
  221.2 0.6 copy-start.11
  221.2 0.7 copy-start.13
  221.2 0.7 copy-start.15
  226.6 257.6 %copy-start.23 = (f32[8,512]{1,0:T(8,128)}, f32[8,512]{1,0:T(8,128)S(1)}, u32[]{:S(2)}) copy-start(f32[8,512]{1,0:T(8,128)S(1)} %get-tuple-element.100) | copy-start | bytes 49156
  464.0 14.2 copy-start.38
  476.9 1.3 copy-start.41
  484.2 136.2 %reduce-scatter.13.cloned.1.call-start = ((), (), s32[]{:S(2)}) async-start(), calls=%async_computation.16 | async-start | bytes 5242880 | tf_op jit(solution)/shard_map/reduce_scatter | solution.py:215
  484.2 6.4 copy-start
  489.0 4.9 copy-start.25
  500.6 4.5 copy-start.10
  500.6 4.5 copy-start.14
  500.6 4.5 copy-start.16
  505.2 0.9 copy-start.12
  506.0 1.5 copy-start.18
  506.0 1.5 copy-start.20
  521.6 0.7 copy-start.40
  521.7 12.5 copy-start.24
  521.7 12.5 copy-start.26
  521.7 100.6 %reduce-scatter.11.cloned.1.call-start = ((), (), s32[]{:S(2)}) async-start(), calls=%async_computation.14 | async-start | bytes 2621440 | tf_op jit(solution)/shard_map/reduce_scatter | solution.py:146
  534.1 111.3 %reduce-scatter.9.cloned.1.call-start = ((), (), s32[]{:S(2)}) async-start(), calls=%async_computation.11 | async-start | bytes 5242880 | tf_op jit(solution)/shard_map/reduce_scatter | solution.py:144
  534.2 5.8 copy-start.5
  539.2 0.8 copy-start.7
  543.2 1.0 copy-start.8
  543.3 5.9 copy-start.2
  543.3 5.9 copy-start.3
  543.3 5.9 copy-start.4
  543.3 195.9 %reduce-scatter.19.cloned.1.call-start = ((), (), s32[]{:S(2)}) async-start(), calls=%async_computation.19 | async-start | bytes 4718592 | tf_op jit(solution)/shard_map/reduce_scatter | solution.py:156
  549.2 402.1 %reduce-scatter.17.cloned.1.call-start = ((), (), s32[]{:S(2)}) async-start(), calls=%async_computation.18 | async-start | bytes 14155776 | tf_op jit(solution)/shard_map/reduce_scatter | solution.py:237
  557.4 680.5 %reduce-scatter.23.cloned.1.call-start = ((), (), s32[]{:S(2)}) async-start(), calls=%async_computation.21 | async-start | bytes 18874368 | tf_op jit(solution)/shard_map/reduce_scatter | solution.py:157
  571.8 952.0 %reduce-scatter.21.cloned.1.call-start = ((), (), s32[]{:S(2)}) async-start(), calls=%async_computation.20 | async-start | bytes 18874368 | tf_op jit(solution)/shard_map/reduce_scatter | solution.py:238
  584.6 0.7 copy-start.32
  584.6 35.7 %copy-start.1 = (bf16[128,2048]{1,0:T(8,128)(2,1)S(1)}, bf16[128,2048]{1,0:T(8,128)(2,1)}, u32[]{:S(2)}) copy-start(bf16[128,2048]{1,0:T(8,128)(2,1)} %param.13) | copy-start | bytes 1572868
  584.6 35.7 %copy-start.22 = (f32[2048]{0:T(1024)S(1)}, f32[2048]{0:T(1024)}, u32[]{:S(2)}) copy-start(f32[2048]{0:T(1024)} %param.14) | copy-start | bytes 24580
  584.7 35.7 %copy-start.28 = (f32[128]{0:T(128)S(1)}, f32[128]{0:T(128)}, u32[]{:S(2)}) copy-start(f32[128]{0:T(128)} %copy-done.27) | copy-start | bytes 1540
  584.7 35.7 %copy-start.35 = (f32[128]{0:T(128)S(1)}, f32[128]{0:T(128)}, u32[]{:S(2)}) copy-start(f32[128]{0:T(128)} %copy-done.34) | copy-start | bytes 1540
  584.7 37.5 %copy-start.37 = (f32[128]{0:T(128)S(1)}, f32[128]{0:T(128)}, u32[]{:S(2)}) copy-start(f32[128]{0:T(128)} %copy-done.36) | copy-start | bytes 1540
  584.7 60.8 %copy-start.29 = (f32[2048]{0:T(1024)S(1)}, f32[2048]{0:T(1024)}, u32[]{:S(2)}) copy-start(f32[2048]{0:T(1024)} %param.23) | copy-start | bytes 24580
  584.7 60.8 %copy-start.30 = (f32[2048]{0:T(1024)S(1)}, f32[2048]{0:T(1024)}, u32[]{:S(2)}) copy-start(f32[2048]{0:T(1024)} %param.19) | copy-start | bytes 24580
  584.7 63.9 %copy-start.6 = (bf16[128,2048]{1,0:T(8,128)(2,1)S(1)}, bf16[128,2048]{1,0:T(8,128)(2,1)}, u32[]{:S(2)}) copy-start(bf16[128,2048]{1,0:T(8,128)(2,1)} %param.25) | copy-start | bytes 1572868
  691.6 832.9 %copy-start.33 = (f32[2048]{0:T(1024)}, f32[2048]{0:T(1024)S(1)}, u32[]{:S(2)}) copy-start(f32[2048]{0:T(1024)S(1)} %get-tuple-element.129) | copy-start | bytes 24580
Sparse Core Ops, SparseCore 0:
  9.6 25.2 all-gather.16
  36.9 51.1 all-gather.10
  90.3 20.7 all-gather.6
  113.5 99.9 all-gather.8
  215.5 123.0 all-gather.12
  340.4 123.5 all-gather.14
  484.3 29.5 reduce-scatter.14
  521.8 42.5 reduce-scatter.12
  566.9 31.4 reduce-scatter.10
  600.9 44.4 reduce-scatter.8
  649.7 89.4 reduce-scatter.18
  743.7 207.5 reduce-scatter.16
  956.1 281.7 reduce-scatter.22
  1242.1 281.7 reduce-scatter.20
where the time goes:
time: 1540 us; the launch traced here: 1530 us
  waiting for transfers between devices  1270 us (82%)
  matrix products  124 us (8%)
  blocking collectives  76.7 us (5%)
  other arithmetic  25 us (2%)
  local copies, waits for them, and re-layouts  15.8 us (1%)
    reduce_scatter x1, waiting for transfers between devices, body(): lax.psum_scatter(down_grad_local, 'fsdp', scatter_dimension=1, tiled=True)  287 us
    reduce_scatter x1, waiting for transfers between devices, body(): lax.psum_scatter(up_grad_local, 'fsdp', scatter_dimension=0, tiled=True)  286 us
    reduce_scatter x1, waiting for transfers between devices, body(): lax.psum_scatter(qkv_grad_local, 'fsdp', scatter_dimension=0, tiled=True)  212 us
    all_gather x1, waiting for transfers between devices, body(): lax.all_gather(w_fc2, 'fsdp', axis=1, tiled=True)  115 us
    all_gather x1, waiting for transfers between devices, body(): lax.all_gather(w_fc1, 'fsdp', axis=0, tiled=True)  112 us
    all_gather x1, waiting for transfers between devices, body(): lax.all_gather(w_qkv, 'fsdp', axis=0, tiled=True)  102 us
    all_gather x1, waiting for transfers between devices, body(): lax.all_gather(w_dense, 'fsdp', axis=1, tiled=True)  53.2 us
    reduce_scatter x1, waiting for transfers between devices, body(): lax.psum_scatter(dense_grad_local, 'fsdp', scatter_dimension=1, tiled=True)  47.6 us
  transfers between devices with their start and end apart: 14, of which 11 were waited for; matrix products, arithmetic and copies ran while one was open for 9% of the time, Pallas kernels for 0%

commit v1 on v0

--- a/solution.py
+++ b/solution.py
@@ -7,6 +7,24 @@
 HEAD_DIM = 64
 ROT = 32
 EPS = 1e-05
+
+
+def collect(shard, axis, dim):
+    ways, here, hop = (lax.axis_size(axis), lax.axis_index(axis), shard.shape[dim])
+    shape = [n * ways if d == dim else n for d, n in enumerate(shard.shape)]
+    full = lax.dynamic_update_slice_in_dim(
+        jnp.zeros(shape, shard.dtype), shard, here * hop, axis=dim
+    )
+    going_up = going_down = shard
+    for far in range(1, ways // 2 + 1):
+        going_up = lax.ppermute(going_up, axis, [(d, (d + 1) % ways) for d in range(ways)])
+        full = lax.dynamic_update_slice_in_dim(full, going_up, (here - far) % ways * hop, axis=dim)
+        if 2 * far < ways:
+            going_down = lax.ppermute(going_down, axis, [(d, (d - 1) % ways) for d in range(ways)])
+            full = lax.dynamic_update_slice_in_dim(
+                full, going_down, (here + far) % ways * hop, axis=dim
+            )
+    return full
 
 
 def layer_norm(values, norm_gain, norm_shift):
@@ -92,7 +110,7 @@
     normed_all = lax.all_gather(normed.astype(jnp.bfloat16), "tensor", axis=0, tiled=True)
     seq_len = normed_all.shape[0]
     qkv_weights, up_weights = (
-        lax.all_gather(w_qkv, "fsdp", axis=0, tiled=True),
+        collect(w_qkv, "fsdp", 0),
         lax.all_gather(w_fc1, "fsdp", axis=0, tiled=True),
     )
     local_width = b_qkv.shape[1]

time: 1540 us -> 1450 us (0.942)
  waiting for transfers between devices: 1270 us -> 1170 us
  starting transfers between devices: 1.03 us -> 21.2 us
    ppermute x0 -> x7, waiting for transfers between devices: none -> 114 us  [the longest x4 114 us: collect(): lax.ppermute(going_up, axis, [(d, (d + 1) % ways) for d in range(ways)])]
    all_gather x1 -> x0, waiting for transfers between devices: 102 us -> none  [body(): lax.all_gather(w_qkv, 'fsdp', axis=0, tiled=True)]
    all_gather x1, waiting for transfers between devices: 53.2 us -> 0.02 us  [body(): lax.all_gather(w_dense, 'fsdp', axis=1, tiled=True)]
    all_gather x1, waiting for transfers between devices: 112 us -> 62.4 us  [body(): lax.all_gather(w_fc1, 'fsdp', axis=0, tiled=True)]
    reduce_scatter x1, waiting for transfers between devices: 0.02 us -> 34.2 us  [body(): lax.psum_scatter(mlp_part.astype(jnp.bfloat16), 'tensor', scatter_dimensi...]
    ppermute x0 -> x7, starting transfers between devices: none -> 20.1 us  [the longest x4 10.9 us: collect(): lax.ppermute(going_up, axis, [(d, (d + 1) % ways) for d in range(ways)])]
    all_gather x1, waiting for transfers between devices: 18.7 us -> 0.01 us  [body(): lax.all_gather(normed.astype(jnp.bfloat16), 'tensor', axis=0, tiled=True)]
    reduce_scatter x1, waiting for transfers between devices: 23.2 us -> 7.52 us  [body(): lax.psum_scatter(attn_part, 'tensor', scatter_dimension=0, tiled=True)]
  transfers between devices with their start and end apart: 14 -> 20, of which waited for: 11 -> 12; matrix products, arithmetic and copies ran while one was open for 9% -> 11% of each run, Pallas kernels for 0% -> 0%
where the time goes in v1:
time: 1450 us
  waiting for transfers between devices  1170 us (81%)
  matrix products  121 us (8%)
  blocking collectives  77.2 us (5%)
  local copies, waits for them, and re-layouts  25.1 us (2%)
  starting transfers between devices  21.2 us (1%)
  other arithmetic  20.4 us (1%)
  between operations  14.7 us (1%)
    reduce_scatter x1, waiting for transfers between devices, body(): lax.psum_scatter(down_grad_local, 'fsdp', scatter_dimension=1, tiled=True)  287 us
    reduce_scatter x1, waiting for transfers between devices, body(): lax.psum_scatter(up_grad_local, 'fsdp', scatter_dimension=0, tiled=True)  286 us
    reduce_scatter x1, waiting for transfers between devices, body(): lax.psum_scatter(qkv_grad_local, 'fsdp', scatter_dimension=0, tiled=True)  212 us
    all_gather x1, waiting for transfers between devices, body(): lax.all_gather(w_fc2, 'fsdp', axis=1, tiled=True)  115 us
    ppermute x4, waiting for transfers between devices, collect(): lax.ppermute(going_up, axis, [(d, (d + 1) % ways) for d in range(ways)])  114 us
    all_gather x1, waiting for transfers between devices, body(): lax.all_gather(w_fc1, 'fsdp', axis=0, tiled=True)  62.4 us
    reduce_scatter x1, waiting for transfers between devices, body(): lax.psum_scatter(dense_grad_local, 'fsdp', scatter_dimension=1, tiled=True)  47.1 us
    psum x1, blocking collectives, body(): lax.psum((gain_local, shift_local, jnp.sum(cotangent, axis=0)), ('fsdp',...  41.9 us
  transfers between devices with their start and end apart: 20, of which 12 were waited for; matrix products, arithmetic and copies ran while one was open for 11% of the time, Pallas kernels for 0%

profile of v1, /device:TPU:0, one launch (start us, length us, event | category | flops | bytes accessed | tf_op | source)
XLA Modules:
  0.0 1447.0 jit_solution(16841329107066111813)
XLA Ops:
  7.2 1.3 convert_reduce_fusion.2
  8.5 1.3 fusion.35
  10.4 2.3 fusion.33
  15.4 3.0 collective-permute-start
  18.4 3.1 collective-permute-start.1
  21.5 30.5 %collective-permute-done = bf16[256,3,512]{2,0,1:T(8,128)(2,1)S(1)} collective-permute-done((bf16[256,3,512]{2,0,1:T(8,128)(2,1)S(1)}, bf16[256,3,512]{2,0,1:T(8,128)(2,1)S(1)}, u32[]{:S(2)}, u32[]{:S(2)}) %collective-permute-start) | collective-permute-done | bytes 786464 | tf_op jit(solution)/shard_map/ppermute | solution.py:20
  52.0 2.5 collective-permute-start.2
  54.5 3.0 collective-permute-start.3
  57.5 32.7 %collective-permute-done.2 = bf16[256,3,512]{2,0,1:T(8,128)(2,1)} collective-permute-done((bf16[256,3,512]{2,0,1:T(8,128)(2,1)S(1)}, bf16[256,3,512]{2,0,1:T(8,128)(2,1)}, u32[]{:S(2)}, u32[]{:S(2)}) %collective-permute-start.2) | collective-permute-done | bytes 786464 | tf_op jit(solution)/shard_map/ppermute | solution.py:20
  90.2 2.6 collective-permute-start.4
  92.8 0.8 multiply_cosine_fusion
  93.6 0.9 fusion.40
  94.6 3.0 collective-permute-start.5
  97.6 3.2 broadcast_in_dim.84
  100.8 0.9 constant_dynamic-update-slice_fusion.7
  101.7 34.6 %collective-permute-done.4 = bf16[256,3,512]{2,0,1:T(8,128)(2,1)S(1)} collective-permute-done((bf16[256,3,512]{2,0,1:T(8,128)(2,1)}, bf16[256,3,512]{2,0,1:T(8,128)(2,1)S(1)}, u32[]{:S(2)}, u32[]{:S(2)}) %collective-permute-start.4) | collective-permute-done | bytes 786464 | tf_op jit(solution)/shard_map/ppermute | solution.py:20
  136.3 2.9 collective-permute-start.6
  139.2 0.9 constant_dynamic-update-slice_fusion.6
  140.2 0.9 constant_dynamic-update-slice_fusion.5
  141.1 2.1 constant_dynamic-update-slice_fusion.4
  143.2 0.9 constant_dynamic-update-slice_fusion.3
  144.1 0.9 constant_dynamic-update-slice_fusion.2
  145.1 0.9 constant_dynamic-update-slice_fusion.1
  146.0 16.0 %collective-permute-done.6 = bf16[256,3,512]{2,0,1:T(8,128)(2,1)S(1)} collective-permute-done((bf16[256,3,512]{2,0,1:T(8,128)(2,1)S(1)}, bf16[256,3,512]{2,0,1:T(8,128)(2,1)S(1)}, u32[]{:S(2)}, u32[]{:S(2)}) %collective-permute-start.6) | collective-permute-done | bytes 786464 | tf_op jit(solution)/shard_map/ppermute | solution.py:20
  162.0 0.9 constant_dynamic-update-slice_fusion
  163.0 6.3 fusion.17
  170.2 1.6 fusion.53
  171.8 1.2 fusion
  173.1 2.1 copy-done
  175.8 3.5 convolution_convert_fusion.2
  179.4 5.8 fusion.27
  185.2 2.0 copy.32
  187.3 4.6 multiply_reduce_fusion
  192.0 4.7 multiply_convert_fusion
  197.6 1.4 fusion.24
  199.2 1.0 pad_maximum_fusion.3
  200.2 2.0 copy.30
  202.3 2.2 copy.31
  204.5 8.7 convolution_bitcast_fusion
  213.3 62.4 %all-gather.10.cloned.1.call-done = bf16[2048,2048]{1,0:T(8,128)(2,1)} async-done(((bf16[256,2048]{1,0:T(8,128)(2,1)}), bf16[2048,2048]{1,0:T(8,128)(2,1)}) %all-gather.10.cloned.1.call-update) | async-done | bytes 8388624 | tf_op jit(solution)/shard_map/all_gather | solution.py:114
  275.7 10.5 fusion.55
  286.2 115.0 %all-gather.12.cloned.1.call-done = bf16[2048,2048]{1,0:T(8,128)(2,1)} async-done(((bf16[2048,256]{1,0:T(8,128)(2,1)}), bf16[2048,2048]{1,0:T(8,128)(2,1)}) %all-gather.12.cloned.1.call-update) | async-done | bytes 8388624 | tf_op jit(solution)/shard_map/all_gather | solution.py:158
  401.2 12.2 convert_reduce_fusion
  413.4 1.3 copy-done.42
  414.8 5.8 convolution_convert_fusion
  421.1 5.0 fusion.26
  426.1 0.8 copy-done.8
  426.9 3.3 fusion.54
  430.3 11.1 convolution_convert_fusion.1
  441.4 5.0 fusion.56
  446.5 8.3 fusion.13
  455.1 14.7 %fusion.50 = f32[2048,2048]{1,0:T(8,128)} fusion(bf16[512,2048]{1,0:T(8,128)(2,1)} %all-gather.14.cloned.1.call-done, f32[512,2048]{1,0:T(8,128)} %fusion.55, f32[2048]{0:T(1024)S(1)} %copy-done.41), kind=kOutput, calls=%fused_computation.105 | convolution fusion | flops 4305453056 | bytes 23076864 | tf_op jit(solution)/shard_map/dot_general | solution.py:82
  469.9 12.5 fusion.57
  482.7 35.4 %all-reduce.1 = (f32[3,512]{1,0:T(4,128)}, f32[2048]{0:T(1024)}) all-reduce(f32[3,512]{1,0:T(4,128)S(1)} %convert_reduce_fusion.1, f32[2048]{0:T(1024)S(1)} %get-tuple-element.77), channel_id=1, replica_groups=mesh['fsdp'=8,'tensor'=4] {'fsdp'}, use_global_device_ids=true, to_apply=%region_17.18 | all-reduce | flops 3584 | bytes 28672 | tf_op jit(solution)/shard_map/psum | solution.py:247
  518.1 1.8 fusion.34
  520.0 7.5 reduce-scatter.9.cloned.1.call-done
  527.5 34.2 %reduce-scatter.11.cloned.1.call-done = bf16[128,2048]{1,0:T(8,128)(2,1)} async-done(((bf16[512,2048]{1,0:T(8,128)(2,1)}), bf16[128,2048]{1,0:T(8,128)(2,1)}) %reduce-scatter.11.cloned.1.call-update) | async-done | bytes 524304 | tf_op jit(solution)/shard_map/reduce_scatter | solution.py:164
  561.7 3.2 fusion.52
  564.9 1.2 convert_reduce_fusion.3
  566.1 41.9 %all-reduce = (f32[2048]{0:T(1024)}, f32[2048]{0:T(1024)}, f32[2048]{0:T(1024)S(1)}) all-reduce(f32[2048]{0:T(1024)S(1)} %get-tuple-element.58, f32[2048]{0:T(1024)S(1)} %get-tuple-element.60, f32[2048]{0:T(1024)S(1)} %get-tuple-element.91), channel_id=1, replica_groups=mesh['fsdp'=8,'tensor'=4] {'fsdp','tensor'}, use_global_device_ids=true, to_apply=%region_12.13 | all-reduce | flops 6144 | bytes 49152 | tf_op jit(solution)/shard_map/psum | solution.py:244
  608.0 47.1 %reduce-scatter.19.cloned.1.call-done = f32[512,256]{1,0:T(8,128)} async-done(((f32[512,2048]{1,0:T(8,128)}), f32[512,256]{1,0:T(8,128)}) %reduce-scatter.19.cloned.1.call-update) | async-done | bytes 524304 | tf_op jit(solution)/shard_map/reduce_scatter | solution.py:174
  655.1 212.1 %reduce-scatter.17.cloned.1.call-done = f32[256,3,512]{2,0,1:T(8,128)} async-done(((f32[2048,3,512]{2,0,1:T(8,128)}), f32[256,3,512]{2,0,1:T(8,128)}) %reduce-scatter.17.cloned.1.call-update) | async-done | bytes 1572880 | tf_op jit(solution)/shard_map/reduce_scatter | solution.py:255
  867.2 286.5 %reduce-scatter.23.cloned.1.call-done = f32[2048,256]{1,0:T(8,128)} async-done(((f32[2048,2048]{1,0:T(8,128)}), f32[2048,256]{1,0:T(8,128)}) %reduce-scatter.23.cloned.1.call-update) | async-done | bytes 2097168 | tf_op jit(solution)/shard_map/reduce_scatter | solution.py:175
  1153.7 286.0 %reduce-scatter.21.cloned.1.call-done = f32[256,2048]{1,0:T(8,128)} async-done(((f32[2048,2048]{1,0:T(8,128)}), f32[256,2048]{1,0:T(8,128)}) %reduce-scatter.21.cloned.1.call-update) | async-done | bytes 2097168 | tf_op jit(solution)/shard_map/reduce_scatter | solution.py:256
  (134 shorter events, 7.9 us)
Async XLA Ops:
  7.2 8.2 copy-start.12
  7.2 86.5 %copy-start.33 = (s32[1,512]{1,0:T(1,128)S(1)}, s32[1,512]{1,0:T(1,128)}, u32[]{:S(2)}) copy-start(s32[1,512]{1,0:T(1,128)} %param.24) | copy-start | bytes 6148
  7.2 155.8 %all-gather.6.cloned.1.call-start = ((), (), s32[]{:S(2)}) async-start(), calls=%async_computation.8 | async-start | bytes 2621440 | tf_op jit(solution)/shard_map/all_gather | solution.py:110
  8.5 1.9 copy-start.29
  9.8 0.5 copy-start.37
  10.4 4.9 copy-start.35
  12.7 163.1 %all-gather.14.cloned.1.call-start = ((), (), s32[]{:S(2)}) async-start(), calls=%async_computation.14 | async-start | bytes 2621440 | tf_op jit(solution)/shard_map/all_gather | solution.py:170
  13.4 162.4 %all-gather.8.cloned.1.call-start = ((), (), s32[]{:S(2)}) async-start(), calls=%async_computation.9 | async-start | bytes 2359296 | tf_op jit(solution)/shard_map/all_gather | solution.py:157
  14.1 261.5 %all-gather.10.cloned.1.call-start = ((), (), s32[]{:S(2)}) async-start(), calls=%async_computation.11 | async-start | bytes 9437184 | tf_op jit(solution)/shard_map/all_gather | solution.py:114
  14.7 386.5 %all-gather.12.cloned.1.call-start = ((), (), s32[]{:S(2)}) async-start(), calls=%async_computation.12 | async-start | bytes 9437184 | tf_op jit(solution)/shard_map/all_gather | solution.py:158
  15.3 502.8 %reduce-scatter.13.cloned.1.call-start = ((), (), s32[]{:S(2)}) async-start(), calls=%async_computation.15 | async-start | bytes 5242880 | tf_op jit(solution)/shard_map/reduce_scatter | solution.py:233
  15.4 36.6 %collective-permute-start = (bf16[256,3,512]{2,0,1:T(8,128)(2,1)S(1)}, bf16[256,3,512]{2,0,1:T(8,128)(2,1)S(1)}, u32[]{:S(2)}, u32[]{:S(2)}) collective-permute-start(bf16[256,3,512]{2,0,1:T(8,128)(2,1)S(1)} %copy-done.12), channel_id=1, source_target_pairs={{0,4},{4,8},{8,12},{12,16},{16,20},{20,24},{24,28},{28,0},{1,5},{5... | collective-permute-start | bytes 2359304 | tf_op jit(solution)/shard_map/ppermute | solution.py:20
  18.4 36.1 %collective-permute-start.1 = (bf16[256,3,512]{2,0,1:T(8,128)(2,1)S(1)}, bf16[256,3,512]{2,0,1:T(8,128)(2,1)S(1)}, u32[]{:S(2)}, u32[]{:S(2)}) collective-permute-start(bf16[256,3,512]{2,0,1:T(8,128)(2,1)S(1)} %copy-done.12), channel_id=1, source_target_pairs={{0,28},{4,0},{8,4},{12,8},{16,12},{20,16},{24,20},{28,24},{1,29},{... | collective-permute-start | bytes 2359304 | tf_op jit(solution)/shard_map/ppermute | solution.py:23
  52.0 38.2 %collective-permute-start.2 = (bf16[256,3,512]{2,0,1:T(8,128)(2,1)S(1)}, bf16[256,3,512]{2,0,1:T(8,128)(2,1)}, u32[]{:S(2)}, u32[]{:S(2)}) collective-permute-start(bf16[256,3,512]{2,0,1:T(8,128)(2,1)S(1)} %collective-permute-done), channel_id=1, source_target_pairs={{0,4},{4,8},{8,12},{12,16},{16,20},{20,24},{24,28},{28,0},{1,5},{5... | collective-permute-start | bytes 2359304 | tf_op jit(solution)/shard_map/ppermute | solution.py:20
  54.5 40.1 %collective-permute-start.3 = (bf16[256,3,512]{2,0,1:T(8,128)(2,1)S(1)}, bf16[256,3,512]{2,0,1:T(8,128)(2,1)S(1)}, u32[]{:S(2)}, u32[]{:S(2)}) collective-permute-start(bf16[256,3,512]{2,0,1:T(8,128)(2,1)S(1)} %collective-permute-done.1), channel_id=1, source_target_pairs={{0,28},{4,0},{8,4},{12,8},{16,12},{20,16},{24,20},{28,24},{1,29},{... | collective-permute-start | bytes 2359304 | tf_op jit(solution)/shard_map/ppermute | solution.py:23
  90.2 46.1 %collective-permute-start.4 = (bf16[256,3,512]{2,0,1:T(8,128)(2,1)}, bf16[256,3,512]{2,0,1:T(8,128)(2,1)S(1)}, u32[]{:S(2)}, u32[]{:S(2)}) collective-permute-start(bf16[256,3,512]{2,0,1:T(8,128)(2,1)} %collective-permute-done.2), channel_id=1, source_target_pairs={{0,4},{4,8},{8,12},{12,16},{16,20},{20,24},{24,28},{28,0},{1,5},{5... | collective-permute-start | bytes 2359304 | tf_op jit(solution)/shard_map/ppermute | solution.py:20
  94.6 50.5 %collective-permute-start.5 = (bf16[256,3,512]{2,0,1:T(8,128)(2,1)S(1)}, bf16[256,3,512]{2,0,1:T(8,128)(2,1)S(1)}, u32[]{:S(2)}, u32[]{:S(2)}) collective-permute-start(bf16[256,3,512]{2,0,1:T(8,128)(2,1)S(1)} %collective-permute-done.3), channel_id=1, source_target_pairs={{0,28},{4,0},{8,4},{12,8},{16,12},{20,16},{24,20},{28,24},{1,29},{... | collective-permute-start | bytes 2359304 | tf_op jit(solution)/shard_map/ppermute | solution.py:23
  136.3 25.7 %collective-permute-start.6 = (bf16[256,3,512]{2,0,1:T(8,128)(2,1)S(1)}, bf16[256,3,512]{2,0,1:T(8,128)(2,1)S(1)}, u32[]{:S(2)}, u32[]{:S(2)}) collective-permute-start(bf16[256,3,512]{2,0,1:T(8,128)(2,1)S(1)} %collective-permute-done.4), channel_id=1, source_target_pairs={{0,4},{4,8},{8,12},{12,16},{16,20},{20,24},{24,28},{28,0},{1,5},{5... | collective-permute-start | bytes 2359304 | tf_op jit(solution)/shard_map/ppermute | solution.py:20
  141.1 21.9 %copy-start.40 = (f32[3,512]{1,0:T(4,128)S(1)}, f32[3,512]{1,0:T(4,128)}, u32[]{:S(2)}) copy-start(f32[3,512]{1,0:T(4,128)} %param.17) | copy-start | bytes 18436
  169.2 0.8 copy-start.19
  169.2 0.8 copy-start.21
  169.3 1.0 copy-start.23
  169.6 2.2 copy-start.10
  170.2 1.6 copy-start.13
  170.2 1.6 copy-start.15
  170.2 1.6 copy-start.17
  171.8 3.3 copy-start
  171.8 3.3 copy-start.25
  175.2 0.6 copy-start.27
  179.4 5.9 copy-start.2
  191.9 4.7 copy-start.11
  191.9 4.7 copy-start.16
  191.9 4.7 copy-start.18
  196.7 0.9 copy-start.14
  197.5 1.5 copy-start.20
  197.5 1.5 copy-start.22
  213.2 188.0 %copy-start.41 = (f32[2048]{0:T(1024)S(1)}, f32[2048]{0:T(1024)}, u32[]{:S(2)}) copy-start(f32[2048]{0:T(1024)} %param.21) | copy-start | bytes 24580
  213.2 304.9 %reduce-scatter.15.cloned.1.call-start = ((), (), s32[]{:S(2)}) async-start(), calls=%async_computation.16 | async-start | bytes 2621440 | tf_op jit(solution)/shard_map/reduce_scatter | solution.py:235
  401.2 13.6 copy-start.39
  413.4 1.3 copy-start.42
  414.8 6.3 copy-start.26
  414.8 6.3 copy-start.28
  420.6 106.9 %reduce-scatter.9.cloned.1.call-start = ((), (), s32[]{:S(2)}) async-start(), calls=%async_computation.10 | async-start | bytes 5242880 | tf_op jit(solution)/shard_map/reduce_scatter | solution.py:162
  421.1 5.8 copy-start.6
  426.1 0.8 copy-start.8
  430.2 11.2 copy-start.9
  430.2 131.4 %reduce-scatter.11.cloned.1.call-start = ((), (), s32[]{:S(2)}) async-start(), calls=%async_computation.13 | async-start | bytes 2621440 | tf_op jit(solution)/shard_map/reduce_scatter | solution.py:164
  441.3 5.2 copy-start.3
  441.4 5.2 copy-start.4
  441.4 5.2 copy-start.5
  441.4 213.7 %reduce-scatter.19.cloned.1.call-start = ((), (), s32[]{:S(2)}) async-start(), calls=%async_computation.18 | async-start | bytes 4718592 | tf_op jit(solution)/shard_map/reduce_scatter | solution.py:174
  446.4 420.7 %reduce-scatter.17.cloned.1.call-start = ((), (), s32[]{:S(2)}) async-start(), calls=%async_computation.17 | async-start | bytes 14155776 | tf_op jit(solution)/shard_map/reduce_scatter | solution.py:255
  454.9 698.9 %reduce-scatter.23.cloned.1.call-start = ((), (), s32[]{:S(2)}) async-start(), calls=%async_computation.20 | async-start | bytes 18874368 | tf_op jit(solution)/shard_map/reduce_scatter | solution.py:175
  469.8 969.9 %reduce-scatter.21.cloned.1.call-start = ((), (), s32[]{:S(2)}) async-start(), calls=%async_computation.19 | async-start | bytes 18874368 | tf_op jit(solution)/shard_map/reduce_scatter | solution.py:256
  482.4 35.7 %copy-start.1 = (bf16[128,2048]{1,0:T(8,128)(2,1)S(1)}, bf16[128,2048]{1,0:T(8,128)(2,1)}, u32[]{:S(2)}) copy-start(bf16[128,2048]{1,0:T(8,128)(2,1)} %param.13) | copy-start | bytes 1572868
  482.4 35.7 %copy-start.24 = (f32[2048]{0:T(1024)S(1)}, f32[2048]{0:T(1024)}, u32[]{:S(2)}) copy-start(f32[2048]{0:T(1024)} %param.14) | copy-start | bytes 24580
  482.4 35.7 %copy-start.30 = (f32[128]{0:T(128)S(1)}, f32[128]{0:T(128)}, u32[]{:S(2)}) copy-start(f32[128]{0:T(128)} %copy-done.29) | copy-start | bytes 1540
  482.4 35.7 %copy-start.36 = (f32[128]{0:T(128)S(1)}, f32[128]{0:T(128)}, u32[]{:S(2)}) copy-start(f32[128]{0:T(128)} %copy-done.35) | copy-start | bytes 1540
  482.4 37.6 %copy-start.38 = (f32[128]{0:T(128)S(1)}, f32[128]{0:T(128)}, u32[]{:S(2)}) copy-start(f32[128]{0:T(128)} %copy-done.37) | copy-start | bytes 1540
  482.4 79.2 %copy-start.31 = (f32[2048]{0:T(1024)S(1)}, f32[2048]{0:T(1024)}, u32[]{:S(2)}) copy-start(f32[2048]{0:T(1024)} %param.23) | copy-start | bytes 24580
  482.4 79.2 %copy-start.32 = (f32[2048]{0:T(1024)S(1)}, f32[2048]{0:T(1024)}, u32[]{:S(2)}) copy-start(f32[2048]{0:T(1024)} %param.19) | copy-start | bytes 24580
  482.5 82.4 %copy-start.7 = (bf16[128,2048]{1,0:T(8,128)(2,1)S(1)}, bf16[128,2048]{1,0:T(8,128)(2,1)}, u32[]{:S(2)}) copy-start(bf16[128,2048]{1,0:T(8,128)(2,1)} %param.25) | copy-start | bytes 1572868
  607.9 832.4 %copy-start.34 = (f32[2048]{0:T(1024)}, f32[2048]{0:T(1024)S(1)}, u32[]{:S(2)}) copy-start(f32[2048]{0:T(1024)S(1)} %get-tuple-element.129) | copy-start | bytes 24580
Sparse Core Ops, SparseCore 0:
  12.8 25.2 all-gather.5
  39.7 22.5 all-gather.13
  64.3 77.0 all-gather.7
  143.4 132.2 all-gather.9
  277.6 123.5 all-gather.11
  403.6 42.6 reduce-scatter.12
  449.0 31.4 reduce-scatter.14
  483.0 44.4 reduce-scatter.8
  530.2 31.4 reduce-scatter.10
  565.7 89.3 reduce-scatter.18
  659.7 207.4 reduce-scatter.16
  871.9 281.7 reduce-scatter.22
  1158.1 281.6 reduce-scatter.20
